TPU v7x, 32 devices: a whole 2x2x4 slice. The times are simulated.
32 devices in a mesh: dp: 8 (over y, x, core), tensor: 4 (over z).
Axes of the slice: x: 2, y: 2, z: 4, core: 2. Of those that a mesh axis runs over, the one named last changes fastest.
Arguments:
- inputs: bfloat16 [64, 256, 1152], P('dp'), may hold values from -6 to 6
- cotangent: bfloat16 [64, 256, 1152], P('dp'), may hold values from -6 to 6
- counts: int32 [8], P('dp'), may hold values from 1 to 8, as said below
- time_ids: int32 [64], P('dp'), may hold values from 0 to 999
- class_ids: int32 [64], P('dp'), may hold values from 0 to 1000
- time_table: bfloat16 [1000, 1152], replicated, may hold values from -4 to 4
- class_table: bfloat16 [1001, 1152], replicated, may hold values from -4 to 4
- ada_weight: bfloat16 [1152, 6, 1152], P(None, None, 'tensor'), may hold values from -0.1875 to 0.1875
- ada_bias: bfloat16 [6, 1152], P(None, 'tensor'), may hold values from -1.75 to 1.75
- qkv_weight: bfloat16 [1152, 3, 1152], P(None, None, 'tensor'), may hold values from -0.1875 to 0.1875
- qv_bias: bfloat16 [2, 1152], P(None, 'tensor'), may hold values from -1.75 to 1.75
- proj_weight: bfloat16 [1152, 1152], P('tensor'), may hold values from -1.5 to 1.5
- proj_bias: bfloat16 [1152], replicated, may hold values from -1.75 to 1.75
- up_weight: bfloat16 [1152, 4608], P(None, 'tensor'), may hold values from -0.1875 to 0.1875
- up_bias: bfloat16 [4608], P('tensor'), may hold values from -1.75 to 1.75
- down_weight: bfloat16 [4608, 1152], P('tensor'), may hold values from -0.09375 to 0.09375
- down_bias: bfloat16 [1152], replicated, may hold values from -1.75 to 1.75
Outputs:
- outputs: bfloat16 [64, 256, 1152], P('dp')
- grad_inputs: bfloat16 [64, 256, 1152], P('dp')
- grad_time_table: float32 [1000, 1152], replicated
- grad_class_table: float32 [1001, 1152], replicated
- grad_ada_weight: float32 [1152, 6, 1152], P(None, None, 'tensor')
- grad_ada_bias: float32 [6, 1152], P(None, 'tensor')
- grad_qkv_weight: float32 [1152, 3, 1152], P(None, None, 'tensor')
- grad_qv_bias: float32 [2, 1152], P(None, 'tensor')
- grad_proj_weight: float32 [1152, 1152], P('tensor')
- grad_proj_bias: float32 [1152], replicated
- grad_up_weight: float32 [1152, 4608], P(None, 'tensor')
- grad_up_bias: float32 [4608], P('tensor')
- grad_down_weight: float32 [4608, 1152], P('tensor')
- grad_down_bias: float32 [1152], replicated
Inputs may be any that keep to these rules, and one draw needn't show every extreme that they name: Each index of dp holds 8 image slots whose first counts live; at least one index has all 8 live.
All inputs are finite; a program needn't handle non-finite values.
Results may differ from a plain program's by a relative error of at most 0.014.
The roundings to bfloat16 on the way count: a program that leaves them out, or rounds other values in their place, can miss the bound.
Values sent between devices are 32-bit elements; how exact they have to be, the bound alone decides.
No kernel may reach another device: no remote copies, remote signals or barrier semaphores. Data moves between devices by JAX's collectives and lax.ppermute only.
A program may use at most 256 MiB of HBM per device.

v0:
```python
import jax
import jax.numpy as jnp
from jax import lax
from jax.sharding import PartitionSpec as P

HEAD_DIM = 72
EPSILON = 1e-06
GELU_ROOT = 0.7978845608028654
GELU_CUBIC = 0.044715


def norm_parts(values):
    average = jnp.mean(values, axis=-1, keepdims=True)
    centred = values - average
    spread = jnp.mean(centred * centred, axis=-1, keepdims=True)
    inverse = lax.rsqrt(spread + EPSILON)
    return (centred * inverse, inverse)


def norm_back(upstream, normed, inverse):
    first_mean = jnp.mean(upstream, axis=-1, keepdims=True)
    second_mean = jnp.mean(upstream * normed, axis=-1, keepdims=True)
    return inverse * (upstream - first_mean - normed * second_mean)


def gelu_parts(values):
    argument = GELU_ROOT * (values + GELU_CUBIC * values * values * values)
    tangent = jnp.tanh(argument)
    result = 0.5 * values * (1.0 + tangent)
    derivative = 0.5 * (1.0 + tangent) + 0.5 * values * (1.0 - tangent * tangent) * GELU_ROOT * (
        1.0 + 3.0 * GELU_CUBIC * values * values
    )
    return (result, derivative)


def local(
    inputs,
    cotangent,
    counts,
    time_ids,
    class_ids,
    time_table,
    class_table,
    ada_weight,
    ada_bias,
    qkv_weight,
    qv_bias,
    proj_weight,
    proj_bias,
    up_weight,
    up_bias,
    down_weight,
    down_bias,
):
    wide = jnp.float32
    narrow = jnp.bfloat16
    images, length, width = inputs.shape
    local_width = qkv_weight.shape[2]
    heads_here = local_width // HEAD_DIM
    scaling = HEAD_DIM ** (-0.5)
    live = (jnp.arange(images, dtype=jnp.int32) < counts[0]).astype(wide)
    time_levels = jnp.arange(time_table.shape[0], dtype=jnp.int32)
    class_levels = jnp.arange(class_table.shape[0], dtype=jnp.int32)
    time_pick = (time_ids[:, None] == time_levels[None, :]).astype(narrow)
    class_pick = (class_ids[:, None] == class_levels[None, :]).astype(narrow)
    condition = jnp.dot(time_pick, time_table, preferred_element_type=wide) + jnp.dot(
        class_pick, class_table, preferred_element_type=wide
    )
    silu_cond = jax.nn.silu(condition).astype(narrow)
    mod_local = jnp.einsum(
        "gd,dke->gke", silu_cond, ada_weight, preferred_element_type=wide
    ) + ada_bias.astype(wide)
    modulation = lax.all_gather(mod_local, "tensor", axis=2, tiled=True)
    shift_attn = modulation[:, 0, None, :]
    scale_attn = modulation[:, 1, None, :]
    gate_attn = modulation[:, 2, None, :]
    shift_mlp = modulation[:, 3, None, :]
    scale_mlp = modulation[:, 4, None, :]
    gate_mlp = modulation[:, 5, None, :]
    input_wide = inputs.astype(wide)
    normed_attn, inverse_attn = norm_parts(input_wide)
    hidden_attn = (normed_attn * (1.0 + scale_attn) + shift_attn).astype(narrow)
    projected = jnp.einsum("gsd,dke->gske", hidden_attn, qkv_weight, preferred_element_type=wide)
    bias_wide = qv_bias.astype(wide)
    shape_heads = (images, length, heads_here, HEAD_DIM)
    query_heads = (projected[:, :, 0] + bias_wide[0]).astype(narrow).reshape(shape_heads)
    key_heads = projected[:, :, 1].astype(narrow).reshape(shape_heads)
    value_heads = (projected[:, :, 2] + bias_wide[1]).astype(narrow).reshape(shape_heads)
    scores = (
        jnp.einsum("gqhe,gkhe->ghqk", query_heads, key_heads, preferred_element_type=wide) * scaling
    )
    highest = jnp.max(scores, axis=-1, keepdims=True)
    exponent = jnp.exp(scores - highest)
    denominator = jnp.sum(exponent, axis=-1, keepdims=True)
    soft_probs = (exponent / denominator).astype(narrow)
    log_total = highest + jnp.log(denominator)
    heads_out = jnp.einsum("ghqk,gkhe->gqhe", soft_probs, value_heads, preferred_element_type=wide)
    heads_out = heads_out.reshape(images, length, local_width).astype(narrow)
    attn_part = jnp.einsum("gse,ed->gsd", heads_out, proj_weight, preferred_element_type=wide)
    attention = lax.psum(attn_part, "tensor") + proj_bias.astype(wide)
    middle = input_wide + gate_attn * attention
    normed_mlp, inverse_mlp = norm_parts(middle)
    hidden_mlp = (normed_mlp * (1.0 + scale_mlp) + shift_mlp).astype(narrow)
    pre_act = jnp.einsum(
        "gsd,df->gsf", hidden_mlp, up_weight, preferred_element_type=wide
    ) + up_bias.astype(wide)
    gelu_value, gelu_slope = gelu_parts(pre_act)
    activated = gelu_value.astype(narrow)
    mlp_part = jnp.einsum("gsf,fd->gsd", activated, down_weight, preferred_element_type=wide)
    branch = lax.psum(mlp_part, "tensor") + down_bias.astype(wide)
    outputs = ((middle + gate_mlp * branch) * live[:, None, None]).astype(narrow)
    grad_out = cotangent.astype(wide) * live[:, None, None]
    d_gate_mlp = jnp.sum(grad_out * branch, axis=1)
    d_branch = (gate_mlp * grad_out).astype(narrow)
    grad_down_bias = jnp.sum(d_branch, axis=(0, 1), dtype=wide)
    grad_down_weight = jnp.einsum("gsf,gsd->fd", activated, d_branch, preferred_element_type=wide)
    d_activated = jnp.einsum("gsd,fd->gsf", d_branch, down_weight, preferred_element_type=wide)
    d_pre = (d_activated * gelu_slope).astype(narrow)
    grad_up_bias = jnp.sum(d_pre, axis=(0, 1), dtype=wide)
    grad_up_weight = jnp.einsum("gsd,gsf->df", hidden_mlp, d_pre, preferred_element_type=wide)
    grad_down_weight, grad_down_bias, grad_up_weight, grad_up_bias = lax.psum(
        (grad_down_weight, grad_down_bias, grad_up_weight, grad_up_bias), "dp"
    )
    d_mlp_part = jnp.einsum("gsf,df->gsd", d_pre, up_weight, preferred_element_type=wide)
    d_hidden_mlp = lax.psum(d_mlp_part, "tensor")
    d_shift_mlp = jnp.sum(d_hidden_mlp, axis=1)
    d_scale_mlp = jnp.sum(d_hidden_mlp * normed_mlp, axis=1)
    d_middle = grad_out + norm_back(d_hidden_mlp * (1.0 + scale_mlp), normed_mlp, inverse_mlp)
    d_gate_attn = jnp.sum(d_middle * attention, axis=1)
    d_attention = (gate_attn * d_middle).astype(narrow)
    grad_proj_bias = jnp.sum(d_attention, axis=(0, 1), dtype=wide)
    grad_proj_weight = jnp.einsum(
        "gse,gsd->ed", heads_out, d_attention, preferred_element_type=wide
    )
    d_heads = jnp.einsum("gsd,ed->gse", d_attention, proj_weight, preferred_element_type=wide)
    d_heads = d_heads.astype(narrow).reshape(shape_heads)
    scores_again = (
        jnp.einsum("gqhe,gkhe->ghqk", query_heads, key_heads, preferred_element_type=wide) * scaling
    )
    probs_again = jnp.exp(scores_again - log_total)
    d_value = jnp.einsum(
        "ghqk,gqhe->gkhe", probs_again.astype(narrow), d_heads, preferred_element_type=wide
    )
    d_value = d_value.astype(narrow)
    d_probs = jnp.einsum("gqhe,gkhe->ghqk", d_heads, value_heads, preferred_element_type=wide)
    row_inner = jnp.sum(probs_again * d_probs, axis=-1, keepdims=True)
    d_scores = (probs_again * (d_probs - row_inner)).astype(narrow)
    d_query = (
        jnp.einsum("ghqk,gkhe->gqhe", d_scores, key_heads, preferred_element_type=wide) * scaling
    ).astype(narrow)
    d_key = (
        jnp.einsum("ghqk,gqhe->gkhe", d_scores, query_heads, preferred_element_type=wide) * scaling
    ).astype(narrow)
    d_projected = jnp.stack([d_query, d_key, d_value], axis=2).reshape(
        images, length, 3, local_width
    )
    grad_qv_bias = jnp.stack(
        [
            jnp.sum(d_query, axis=(0, 1), dtype=wide).reshape(local_width),
            jnp.sum(d_value, axis=(0, 1), dtype=wide).reshape(local_width),
        ],
        axis=0,
    )
    grad_qkv_weight = jnp.einsum(
        "gsd,gske->dke", hidden_attn, d_projected, preferred_element_type=wide
    )
    d_attn_part = jnp.einsum("gske,dke->gsd", d_projected, qkv_weight, preferred_element_type=wide)
    d_hidden_attn = lax.psum(d_attn_part, "tensor")
    d_shift_attn = jnp.sum(d_hidden_attn, axis=1)
    d_scale_attn = jnp.sum(d_hidden_attn * normed_attn, axis=1)
    grad_inputs = (
        d_middle + norm_back(d_hidden_attn * (1.0 + scale_attn), normed_attn, inverse_attn)
    ).astype(narrow)
    d_modulation = jnp.stack(
        [d_shift_attn, d_scale_attn, d_gate_attn, d_shift_mlp, d_scale_mlp, d_gate_mlp], axis=1
    ).astype(narrow)
    start_column = lax.axis_index("tensor") * local_width
    d_mod_local = lax.dynamic_slice_in_dim(d_modulation, start_column, local_width, 2)
    grad_ada_weight = jnp.einsum("gd,gke->dke", silu_cond, d_mod_local, preferred_element_type=wide)
    grad_ada_bias = jnp.sum(d_mod_local, axis=0, dtype=wide)
    (
        grad_qkv_weight,
        grad_qv_bias,
        grad_proj_weight,
        grad_proj_bias,
        grad_ada_weight,
        grad_ada_bias,
    ) = lax.psum(
        (
            grad_qkv_weight,
            grad_qv_bias,
            grad_proj_weight,
            grad_proj_bias,
            grad_ada_weight,
            grad_ada_bias,
        ),
        "dp",
    )
    sigmoid_cond = jax.nn.sigmoid(condition)
    d_condition = jnp.einsum("gke,dke->gd", d_mod_local, ada_weight, preferred_element_type=wide)
    d_condition = d_condition * sigmoid_cond * (1.0 + condition * (1.0 - sigmoid_cond))
    exact = lax.Precision.HIGHEST
    grad_time_table = jnp.dot(time_pick.astype(wide).T, d_condition, precision=exact)
    grad_class_table = jnp.dot(class_pick.astype(wide).T, d_condition, precision=exact)
    grad_time_table, grad_class_table = lax.psum(
        (grad_time_table, grad_class_table), ("dp", "tensor")
    )
    return (
        outputs,
        grad_inputs,
        grad_time_table,
        grad_class_table,
        grad_ada_weight,
        grad_ada_bias,
        grad_qkv_weight,
        grad_qv_bias,
        grad_proj_weight,
        grad_proj_bias,
        grad_up_weight,
        grad_up_bias,
        grad_down_weight,
        grad_down_bias,
    )


def solution(mesh):
    in_specs = (
        P("dp", None, None),
        P("dp", None, None),
        P("dp"),
        P("dp"),
        P("dp"),
        P(),
        P(),
        P(None, None, "tensor"),
        P(None, "tensor"),
        P(None, None, "tensor"),
        P(None, "tensor"),
        P("tensor", None),
        P(),
        P(None, "tensor"),
        P("tensor"),
        P("tensor", None),
        P(),
    )
    out_specs = (
        P("dp", None, None),
        P("dp", None, None),
        P(),
        P(),
        P(None, None, "tensor"),
        P(None, "tensor"),
        P(None, None, "tensor"),
        P(None, "tensor"),
        P("tensor", None),
        P(),
        P(None, "tensor"),
        P("tensor"),
        P("tensor", None),
        P(),
    )
    return jax.shard_map(local, mesh=mesh, in_specs=in_specs, out_specs=out_specs, check_vma=False)
```

profile of v0, /device:TPU:0, one launch (start us, length us, event | category | flops | bytes accessed | tf_op | source)
XLA Modules:
  0.0 2098.7 jit_solution(2705256795855632784)
XLA Ops:
  10.5 4.5 fusion.14
  19.4 91.1 %all_gather.3 = f32[8,6,1152]{1,0,2:T(8,128)} all-gather(f32[8,6,288]{1,0,2:T(8,128)} %copy.58), channel_id=1, replica_groups=mesh['dp'=8,'tensor'=4] {'tensor'}, dimensions={2}, use_global_device_ids=true | all-gather | bytes 276480 | tf_op jit(solution)/shard_map/all_gather | solution.py:73
  110.5 22.1 %fusion.73 = (f32[8,1,1152]{1,0,2:T(8,128)}, f32[8,1,1152]{1,0,2:T(8,128)}, f32[8,1,1152]{1,0,2:T(8,128)}, f32[8,1,1152]{1,0,2:T(8,128)}, f32[8,1,1152]{1,0,2:T(8,128)}, /*index=5*/f32[8,1,1152]{1,0,2:T(8,128)}) fusion(f32[8,6,1152]{1,0,2:T(8,128)} %all_gather.3), kind=kLoop, calls=%fused_computation.140 | loop fusion | bytes 442368 | tf_op jit(solution)/shard_map/slice | solution.py:79
  139.3 7.8 fusion.40
  159.6 5.4 fusion.49
  180.0 310.3 %all-reduce.10.cloned.1.call-done = f32[8,256,1152]{2,1,0:T(8,128)} async-done(((f32[8,256,1152]{2,1,0:T(8,128)}), f32[8,256,1152]{2,1,0:T(8,128)}) %all-reduce.10.cloned.1.call-update) | async-done | bytes 9437200 | tf_op jit(solution)/shard_map/psum | solution.py:100
  490.3 10.4 fusion.71
  500.7 4.9 multiply_reduce_fusion.4
  507.1 9.6 fusion.35
  516.7 12.8 convert_reduce_fusion.2
  531.8 9.6 fusion.33
  542.2 13.1 fusion.31
  555.3 309.9 %all-reduce.12.cloned.1.call-done = f32[8,256,1152]{2,1,0:T(8,128)} async-done(((f32[8,256,1152]{2,1,0:T(8,128)}), f32[8,256,1152]{2,1,0:T(8,128)}) %all-reduce.12.cloned.1.call-update) | async-done | bytes 9437200 | tf_op jit(solution)/shard_map/psum | solution.py:125
  865.2 8.5 multiply_reduce_fusion.1
  874.4 11.4 convert_reduce_fusion.3
  900.4 7.9 convolution_bitcast_fusion.2
  909.1 16.6 convolution_bitcast_fusion
  925.7 611.2 %all-reduce.18.cloned.1.call-done = (f32[8,256,1152]{2,1,0:T(8,128)}, f32[8,256,1152]{2,1,0:T(8,128)}) async-done(((f32[8,256,1152]{2,1,0:T(8,128)}, f32[8,256,1152]{2,1,0:T(8,128)}), (f32[8,256,1152]{2,1,0:T(8,128)}, f32[8,256,1152]{2,1,0:T(8,128)})) %all-reduce.18.cloned.1.call-update) | async-done | bytes 18874384 | tf_op jit(solution)/shard_map/psum | solution.py:110
  1537.0 8.8 fusion.13
  1545.9 13.2 convert_reduce_fusion.1
  1559.3 9.1 multiply_reduce_fusion.2
  1569.2 4.4 fusion.54
  1573.6 4.3 fusion.53
  1578.4 15.1 convolution_bitcast_fusion.1
  1593.5 5.3 convolution_bitcast_fusion.4
  1598.8 9.8 convolution_bitcast_fusion.3
  1608.6 4.7 fusion.56
  1614.0 24.1 %all-reduce.1 = (f32[6,288]{1,0:T(8,128)}, f32[2,288]{1,0:T(2,128)}, f32[1152]{0:T(1024)}, f32[1152]{0:T(1024)}, f32[1152]{0:T(1024)}) all-reduce(f32[6,288]{1,0:T(8,128)S(1)} %convert_reduce_fusion.6, f32[2,288]{1,0:T(2,128)S(1)} %pad_maximum_fusion.3, f32[1152]{0:T(1024)S(1)} %copy-done.42, ...), channel_id=1, replica_groups=mesh['dp'=8,'tensor'=4] {'dp'}, use_global_device_ids=true, to_apply=%region_25.26 | all-reduce | flops 5760 | bytes 46080 | tf_op jit(solution)/shard_map/psum | solution.py:188
  1638.2 128.6 %all-reduce.14.cloned.1.call-done = (f32[1000,1152]{1,0:T(8,128)}, f32[1001,1152]{1,0:T(8,128)}) async-done(((f32[1000,1152]{1,0:T(8,128)}, f32[1001,1152]{1,0:T(8,128)}), (f32[1000,1152]{1,0:T(8,128)}, f32[1001,1152]{1,0:T(8,128)})) %all-reduce.14.cloned.1.call-update) | async-done | bytes 9220624 | tf_op jit(solution)/shard_map/psum | solution.py:205
  1766.7 300.5 %all-reduce.16.cloned.1.call-done = (f32[1152,6,288]{0,2,1:T(8,128)}, f32[1152,3,288]{0,2,1:T(8,128)}, f32[288,1152]{1,0:T(8,128)}, f32[1152,1152]{1,0:T(8,128)}, f32[1152,1152]{1,0:T(8,128)}) async-done(((f32[1152,6,288]{0,2,1:T(8,128)}, f32[1152,3,288]{0,2,1:T(8,128)}, f32[288,1152]{1,0:T(8,128)}, f32[1152,1152]{1,0:T(8,128)}, f32[1152,1152]{1,0:T(8,128)}), (f32[1152,6,288]{0,2,1:T(8,128)}, ...) | async-done | bytes 23887888 | tf_op jit(solution)/shard_map/psum | solution.py:188
  2067.2 5.1 copy.107
  2076.8 4.0 copy.109
  (231 shorter events, 78.9 us)
Async XLA Ops:
  7.2 509.5 %copy-start = (bf16[1152,1152]{1,0:T(8,128)(2,1)S(1)}, bf16[1152,1152]{1,0:T(8,128)(2,1)}, u32[]{:S(2)}) copy-start(bf16[1152,1152]{1,0:T(8,128)(2,1)} %param.32) | copy-start | bytes 7962628
  7.2 483.1 %all-reduce.10.cloned.1.call-start = ((), (), s32[]{:S(2)}) async-start(), calls=%async_computation | async-start | bytes 18874368 | tf_op jit(solution)/shard_map/psum | solution.py:100
  7.3 9.4 copy-start.6
  10.5 128.8 %copy-start.32 = (f32[8,256]{1,0:T(8,128)}, f32[8,256]{1,0:T(8,128)S(1)}, u32[]{:S(2)}) copy-start(f32[8,256]{1,0:T(8,128)S(1)} %broadcast_multiply_fusion.5) | copy-start | bytes 24580
  15.0 124.3 %copy-start.34 = (f32[8,256]{1,0:T(8,128)}, f32[8,256]{1,0:T(8,128)S(1)}, u32[]{:S(2)}) copy-start(f32[8,256]{1,0:T(8,128)S(1)} %add_rsqrt_fusion.1) | copy-start | bytes 24580
  135.9 11.2 copy-start.38
  165.0 700.2 %all-reduce.12.cloned.1.call-start = ((), (), s32[]{:S(2)}) async-start(), calls=%async_computation.1 | async-start | bytes 18874368 | tf_op jit(solution)/shard_map/psum | solution.py:125
  165.7 324.6 %copy-start.36 = (f32[1152]{0:T(1024)}, f32[1152]{0:T(1024)S(1)}, u32[]{:S(2)}) copy-start(f32[1152]{0:T(1024)S(1)} %convert_element_type.142) | copy-start | bytes 13828
  180.0 336.7 %copy-start.54 = (f32[8]{0:T(128)}, f32[8]{0:T(128)S(1)}, u32[]{:S(2)}) copy-start(f32[8]{0:T(128)S(1)} %compare_convert_fusion) | copy-start | bytes 100
  490.3 15.3 copy-start.57
  500.7 15.9 slice-start.10
  507.1 9.6 slice-start.11
  541.5 995.5 %all-reduce.18.cloned.1.call-start = ((), (), s32[]{:S(2)}) async-start(), calls=%async_computation.4 | async-start | bytes 37748736 | tf_op jit(solution)/shard_map/psum | solution.py:110
  555.3 318.4 %copy-start.55 = (f32[8]{0:T(128)S(1)}, f32[8]{0:T(128)}, u32[]{:S(2)}) copy-start(f32[8]{0:T(128)} %copy-done.54) | copy-start | bytes 100
  908.4 858.3 %all-reduce.14.cloned.1.call-start = ((), (), s32[]{:S(2)}) async-start(), calls=%async_computation.2 | async-start | bytes 18505728 | tf_op jit(solution)/shard_map/psum | solution.py:205
  909.1 627.9 %copy-start.29 = (f32[8,1152]{1,0:T(8,128)S(1)}, f32[8,1152]{1,0:T(8,128)}, u32[]{:S(2)}) copy-start(f32[8,1152]{1,0:T(8,128)} %copy-done.28) | copy-start | bytes 110596
  909.1 627.9 %copy-start.33 = (f32[8,256]{1,0:T(8,128)S(1)}, f32[8,256]{1,0:T(8,128)}, u32[]{:S(2)}) copy-start(f32[8,256]{1,0:T(8,128)} %copy-done.32) | copy-start | bytes 24580
  909.1 627.9 %copy-start.35 = (f32[8,256]{1,0:T(8,128)S(1)}, f32[8,256]{1,0:T(8,128)}, u32[]{:S(2)}) copy-start(f32[8,256]{1,0:T(8,128)} %copy-done.34) | copy-start | bytes 24580
  1537.0 22.2 %slice-start.2 = ((s8[4718592]{0:T(1024)(128)(4,1)}), s8[4194304]{0:T(1024)(128)(4,1)S(1)}, s32[]{:S(2)}) async-start(s8[4718592]{0:T(1024)(128)(4,1)} %bitcast.124), calls=%async_computation.7 | async-start | bytes 8388608
  1537.0 22.2 %slice-start.4 = ((s8[9437184]{0:T(1024)(128)(4,1)}), s8[4194304]{0:T(1024)(128)(4,1)S(1)}, s32[]{:S(2)}) async-start(s8[9437184]{0:T(1024)(128)(4,1)} %bitcast.126), calls=%async_computation.9 | async-start | bytes 8388608
  1537.0 22.2 %slice-start.5 = ((s8[9437184]{0:T(1024)(128)(4,1)}), s8[4194304]{0:T(1024)(128)(4,1)S(1)}, s32[]{:S(2)}) async-start(s8[9437184]{0:T(1024)(128)(4,1)} %bitcast.126), calls=%async_computation.10 | async-start | bytes 8388608
  1537.0 22.2 %slice-start.7 = ((s8[9437184]{0:T(1024)(128)(4,1)}), s8[4194304]{0:T(1024)(128)(4,1)S(1)}, s32[]{:S(2)}) async-start(s8[9437184]{0:T(1024)(128)(4,1)} %bitcast.128), calls=%async_computation.12 | async-start | bytes 8388608
  1537.0 22.2 %slice-start.8 = ((s8[9437184]{0:T(1024)(128)(4,1)}), s8[4194304]{0:T(1024)(128)(4,1)S(1)}, s32[]{:S(2)}) async-start(s8[9437184]{0:T(1024)(128)(4,1)} %bitcast.128), calls=%async_computation.13 | async-start | bytes 8388608
  1545.9 13.3 slice-start.3
  1545.9 13.3 slice-start.6
  1545.9 13.3 slice-start.9
  1545.9 13.3 copy-start.37
  1559.3 9.9 copy-start.51
  1569.2 9.2 copy-start.41
  1577.9 15.6 copy-start.18
  1577.9 489.3 %all-reduce.16.cloned.1.call-start = ((), (), s32[]{:S(2)}) async-start(), calls=%async_computation.3 | async-start | bytes 47775744 | tf_op jit(solution)/shard_map/psum | solution.py:188
  2072.3 12.5 slice-start.16
  (51 other events, 257.0 us)
Sparse Core Ops, SparseCore 0:
  165.1 325.1 all-reduce.9
  541.6 323.5 all-reduce.11
  908.5 628.3 all-reduce.17
  1578.0 188.6 all-reduce.13
  1772.5 294.6 all-reduce.15
where the time goes:
time: 2100 us
  waiting for transfers between devices  1660 us (79%)
  matrix products  144 us (7%)
  blocking collectives  115 us (5%)
  local copies, waits for them, and re-layouts  84.7 us (4%)
  other arithmetic  78.3 us (4%)
    psum x1, waiting for transfers between devices, local(): branch = lax.psum(mlp_part, 'tensor') + down_bias.astype(wide)  611 us
    psum x1, waiting for transfers between devices, local(): attention = lax.psum(attn_part, 'tensor') + proj_bias.astype(wide)  310 us
    psum x1, waiting for transfers between devices, local(): d_hidden_mlp = lax.psum(d_mlp_part, 'tensor')  310 us
    psum x1, waiting for transfers between devices, local(): lax.psum((grad_qkv_weight, grad_qv_bias, grad_proj_weight, grad_proj_bias...  300 us
    psum x1, waiting for transfers between devices, local(): lax.psum((grad_time_table, grad_class_table), ('dp', 'tensor'))  129 us
    all_gather x1, blocking collectives, local(): modulation = lax.all_gather(mod_local, 'tensor', axis=2, tiled=True)  91.1 us
    unnamed x174, local copies, waits for them, and re-layouts  57 us
  transfers between devices with their start and end apart: 5, of which 5 were waited for; matrix products, arithmetic and copies ran while one was open for 4% of the time, Pallas kernels for 0%

commit v1 on v0

--- a/solution.py
+++ b/solution.py
@@ -70,7 +70,15 @@
     mod_local = jnp.einsum(
         "gd,dke->gke", silu_cond, ada_weight, preferred_element_type=wide
     ) + ada_bias.astype(wide)
-    modulation = lax.all_gather(mod_local, "tensor", axis=2, tiled=True)
+    modulation = jnp.concatenate(
+        lax.all_to_all(
+            jnp.stack(lax.axis_size("tensor") * [mod_local]),
+            axis_name="tensor",
+            split_axis=0,
+            concat_axis=0,
+        ),
+        2,
+    )
     shift_attn = modulation[:, 0, None, :]
     scale_attn = modulation[:, 1, None, :]
     gate_attn = modulation[:, 2, None, :]

time: 2100 us -> 2000 us (0.952)
  blocking collectives: 115 us -> 24.2 us
  local copies, waits for them, and re-layouts: 84.7 us -> 39.4 us
    all_gather x1 -> x0, blocking collectives: 91.1 us -> none  [local(): modulation = lax.all_gather(mod_local, 'tensor', axis=2, tiled=True)]
    slice x1 -> x0, local copies, waits for them, and re-layouts: 22.1 us -> none  [local(): gate_mlp = modulation[:, 5, None, :]]
    unnamed x174 -> x156, local copies, waits for them, and re-layouts: 57 us -> 37.4 us
  transfers between devices with their start and end apart: 5 -> 6, of which waited for: 5 -> 6; matrix products, arithmetic and copies ran while one was open for 4% -> 4% of each run, Pallas kernels for 0% -> 0%
where the time goes in v1:
time: 2000 us; the launch traced here: 1990 us
  waiting for transfers between devices  1680 us (84%)
  matrix products  146 us (7%)
  other arithmetic  79.2 us (4%)
  local copies, waits for them, and re-layouts  39.4 us (2%)
  blocking collectives  24.2 us (1%)
    psum x1, waiting for transfers between devices, local(): branch = lax.psum(mlp_part, 'tensor') + down_bias.astype(wide)  611 us
    psum x1, waiting for transfers between devices, local(): attention = lax.psum(attn_part, 'tensor') + proj_bias.astype(wide)  323 us
    psum x1, waiting for transfers between devices, local(): d_hidden_mlp = lax.psum(d_mlp_part, 'tensor')  310 us
    psum x1, waiting for transfers between devices, local(): lax.psum((grad_qkv_weight, grad_qv_bias, grad_proj_weight, grad_proj_bias...  300 us
    psum x1, waiting for transfers between devices, local(): lax.psum((grad_time_table, grad_class_table), ('dp', 'tensor'))  129 us
  transfers between devices with their start and end apart: 6, of which 6 were waited for; matrix products, arithmetic and copies ran while one was open for 4% of the time, Pallas kernels for 0%

profile of v1, /device:TPU:0, one launch (start us, length us, event | category | flops | bytes accessed | tf_op | source)
XLA Modules:
  0.0 1988.1 jit_solution(2790765325607285916)
XLA Ops:
  12.9 3.5 convolution_add_fusion.1
  17.2 6.3 all-to-all-start
  26.6 3.7 fusion.14
  34.7 7.8 fusion.40
  50.8 5.2 fusion.49
  57.2 322.6 %all-reduce.10.cloned.1.call-done = f32[8,256,1152]{2,1,0:T(8,128)} async-done(((f32[8,256,1152]{2,1,0:T(8,128)}), f32[8,256,1152]{2,1,0:T(8,128)}) %all-reduce.10.cloned.1.call-update) | async-done | bytes 9437200 | tf_op jit(solution)/shard_map/psum | solution.py:108
  379.9 10.4 fusion.73
  390.3 4.9 multiply_reduce_fusion.4
  396.7 9.6 fusion.35
  406.3 12.8 convert_reduce_fusion.2
  421.3 9.2 fusion.33
  430.8 13.1 fusion.31
  444.0 310.4 %all-reduce.12.cloned.1.call-done = f32[8,256,1152]{2,1,0:T(8,128)} async-done(((f32[8,256,1152]{2,1,0:T(8,128)}), f32[8,256,1152]{2,1,0:T(8,128)}) %all-reduce.12.cloned.1.call-update) | async-done | bytes 9437200 | tf_op jit(solution)/shard_map/psum | solution.py:133
  754.4 8.5 multiply_reduce_fusion.1
  763.5 11.4 convert_reduce_fusion.3
  789.6 7.9 convolution_bitcast_fusion.2
  798.3 16.6 convolution_bitcast_fusion
  814.9 611.2 %all-reduce.18.cloned.1.call-done = (f32[8,256,1152]{2,1,0:T(8,128)}, f32[8,256,1152]{2,1,0:T(8,128)}) async-done(((f32[8,256,1152]{2,1,0:T(8,128)}, f32[8,256,1152]{2,1,0:T(8,128)}), (f32[8,256,1152]{2,1,0:T(8,128)}, f32[8,256,1152]{2,1,0:T(8,128)})) %all-reduce.18.cloned.1.call-update) | async-done | bytes 18874384 | tf_op jit(solution)/shard_map/psum | solution.py:118
  1426.2 9.1 fusion.13
  1435.3 13.2 convert_reduce_fusion.1
  1448.7 9.1 multiply_reduce_fusion.2
  1458.6 4.4 fusion.56
  1463.0 4.3 fusion.55
  1467.6 15.1 convolution_bitcast_fusion.1
  1482.7 5.3 convolution_bitcast_fusion.4
  1488.0 9.9 convolution_bitcast_fusion.3
  1497.8 4.7 fusion.58
  1503.2 24.2 %all-reduce.1 = (f32[6,288]{1,0:T(8,128)}, f32[2,288]{1,0:T(2,128)}, f32[1152]{0:T(1024)}, f32[1152]{0:T(1024)}, f32[1152]{0:T(1024)}) all-reduce(f32[6,288]{1,0:T(8,128)S(1)} %convert_reduce_fusion.6, f32[2,288]{1,0:T(2,128)S(1)} %pad_maximum_fusion.3, f32[1152]{0:T(1024)S(1)} %copy-done.39, ...), channel_id=1, replica_groups=mesh['dp'=8,'tensor'=4] {'dp'}, use_global_device_ids=true, to_apply=%region_25.26 | all-reduce | flops 5760 | bytes 46080 | tf_op jit(solution)/shard_map/psum | solution.py:196
  1527.5 128.7 %all-reduce.14.cloned.1.call-done = (f32[1000,1152]{1,0:T(8,128)}, f32[1001,1152]{1,0:T(8,128)}) async-done(((f32[1000,1152]{1,0:T(8,128)}, f32[1001,1152]{1,0:T(8,128)}), (f32[1000,1152]{1,0:T(8,128)}, f32[1001,1152]{1,0:T(8,128)})) %all-reduce.14.cloned.1.call-update) | async-done | bytes 9220624 | tf_op jit(solution)/shard_map/psum | solution.py:213
  1656.1 300.5 %all-reduce.16.cloned.1.call-done = (f32[1152,6,288]{0,2,1:T(8,128)}, f32[1152,3,288]{0,2,1:T(8,128)}, f32[288,1152]{1,0:T(8,128)}, f32[1152,1152]{1,0:T(8,128)}, f32[1152,1152]{1,0:T(8,128)}) async-done(((f32[1152,6,288]{0,2,1:T(8,128)}, f32[1152,3,288]{0,2,1:T(8,128)}, f32[288,1152]{1,0:T(8,128)}, f32[1152,1152]{1,0:T(8,128)}, f32[1152,1152]{1,0:T(8,128)}), (f32[1152,6,288]{0,2,1:T(8,128)}, ...) | async-done | bytes 23887888 | tf_op jit(solution)/shard_map/psum | solution.py:196
  1956.6 5.1 copy.88
  1966.2 4.0 copy.90
  (214 shorter events, 59.8 us)
Async XLA Ops:
  7.2 399.1 %copy-start = (bf16[1152,1152]{1,0:T(8,128)(2,1)S(1)}, bf16[1152,1152]{1,0:T(8,128)(2,1)}, u32[]{:S(2)}) copy-start(bf16[1152,1152]{1,0:T(8,128)(2,1)} %param.32) | copy-start | bytes 7962628
  7.2 16.3 copy-start.50
  17.2 16.0 all-to-all-start
  23.5 356.4 %all-reduce.10.cloned.1.call-start = ((), (), s32[]{:S(2)}) async-start(), calls=%async_computation.1 | async-start | bytes 18874368 | tf_op jit(solution)/shard_map/psum | solution.py:108
  26.6 15.9 copy-start.29
  30.4 17.1 copy-start.41
  30.5 12.0 copy-start.31
  56.0 698.4 %all-reduce.12.cloned.1.call-start = ((), (), s32[]{:S(2)}) async-start(), calls=%async_computation.2 | async-start | bytes 18874368 | tf_op jit(solution)/shard_map/psum | solution.py:133
  57.2 333.1 %copy-start.33 = (f32[1152]{0:T(1024)}, f32[1152]{0:T(1024)S(1)}, u32[]{:S(2)}) copy-start(f32[1152]{0:T(1024)S(1)} %convert_element_type.142) | copy-start | bytes 13828
  57.2 349.0 %copy-start.48 = (f32[8]{0:T(128)}, f32[8]{0:T(128)S(1)}, u32[]{:S(2)}) copy-start(f32[8]{0:T(128)S(1)} %compare_convert_fusion) | copy-start | bytes 100
  379.9 15.4 copy-start.51
  390.3 15.9 slice-start.10
  396.7 9.6 slice-start.11
  430.6 995.5 %all-reduce.18.cloned.1.call-start = ((), (), s32[]{:S(2)}) async-start(), calls=%async_computation.5 | async-start | bytes 37748736 | tf_op jit(solution)/shard_map/psum | solution.py:118
  444.0 318.9 %copy-start.49 = (f32[8]{0:T(128)S(1)}, f32[8]{0:T(128)}, u32[]{:S(2)}) copy-start(f32[8]{0:T(128)} %copy-done.48) | copy-start | bytes 100
  797.6 858.5 %all-reduce.14.cloned.1.call-start = ((), (), s32[]{:S(2)}) async-start(), calls=%async_computation.3 | async-start | bytes 18505728 | tf_op jit(solution)/shard_map/psum | solution.py:213
  798.3 627.9 %copy-start.28 = (f32[8,1152]{1,0:T(8,128)S(1)}, f32[8,1152]{1,0:T(8,128)}, u32[]{:S(2)}) copy-start(f32[8,1152]{1,0:T(8,128)} %copy-done.27) | copy-start | bytes 110596
  798.3 627.9 %copy-start.30 = (f32[8,256]{1,0:T(8,128)S(1)}, f32[8,256]{1,0:T(8,128)}, u32[]{:S(2)}) copy-start(f32[8,256]{1,0:T(8,128)} %copy-done.29) | copy-start | bytes 24580
  798.3 627.9 %copy-start.32 = (f32[8,256]{1,0:T(8,128)S(1)}, f32[8,256]{1,0:T(8,128)}, u32[]{:S(2)}) copy-start(f32[8,256]{1,0:T(8,128)} %copy-done.31) | copy-start | bytes 24580
  1426.1 22.4 %slice-start.2 = ((s8[4718592]{0:T(1024)(128)(4,1)}), s8[4194304]{0:T(1024)(128)(4,1)S(1)}, s32[]{:S(2)}) async-start(s8[4718592]{0:T(1024)(128)(4,1)} %bitcast.131), calls=%async_computation.8 | async-start | bytes 8388608
  1426.1 22.4 %slice-start.4 = ((s8[9437184]{0:T(1024)(128)(4,1)}), s8[4194304]{0:T(1024)(128)(4,1)S(1)}, s32[]{:S(2)}) async-start(s8[9437184]{0:T(1024)(128)(4,1)} %bitcast.133), calls=%async_computation.10 | async-start | bytes 8388608
  1426.2 22.4 %slice-start.5 = ((s8[9437184]{0:T(1024)(128)(4,1)}), s8[4194304]{0:T(1024)(128)(4,1)S(1)}, s32[]{:S(2)}) async-start(s8[9437184]{0:T(1024)(128)(4,1)} %bitcast.133), calls=%async_computation.11 | async-start | bytes 8388608
  1426.2 22.4 %slice-start.7 = ((s8[9437184]{0:T(1024)(128)(4,1)}), s8[4194304]{0:T(1024)(128)(4,1)S(1)}, s32[]{:S(2)}) async-start(s8[9437184]{0:T(1024)(128)(4,1)} %bitcast.135), calls=%async_computation.13 | async-start | bytes 8388608
  1426.2 22.4 %slice-start.8 = ((s8[9437184]{0:T(1024)(128)(4,1)}), s8[4194304]{0:T(1024)(128)(4,1)S(1)}, s32[]{:S(2)}) async-start(s8[9437184]{0:T(1024)(128)(4,1)} %bitcast.135), calls=%async_computation.14 | async-start | bytes 8388608
  1435.3 13.3 slice-start.3
  1435.3 13.3 slice-start.6
  1435.3 13.3 slice-start.9
  1435.3 13.3 copy-start.34
  1448.7 9.9 copy-start.46
  1467.3 15.3 copy-start.17
  1467.3 489.3 %all-reduce.16.cloned.1.call-start = ((), (), s32[]{:S(2)}) async-start(), calls=%async_computation.4 | async-start | bytes 47775744 | tf_op jit(solution)/shard_map/psum | solution.py:196
  1961.7 12.5 slice-start.16
  (46 other events, 211.8 us)
Sparse Core Ops, SparseCore 0:
  56.1 323.7 all-reduce.9
  430.7 323.6 all-reduce.11
  797.7 628.3 all-reduce.17
  1467.4 188.6 all-reduce.13
  1661.9 294.6 all-reduce.15
